TPU v7x, 32 devices: a whole 2x2x4 slice. The times are simulated.
32 devices in a mesh: dom: 8 (over y, x, core), sub: 4 (over z).
Axes of the slice: x: 2, y: 2, z: 4, core: 2. Of those that a mesh axis runs over, the one named last changes fastest.
Arguments:
- start_dofs: float32 [140, 8192], P(None, ('dom', 'sub')), may hold values from -6 to 6
- inv_jac: float32 [9, 8192], P(None, ('dom', 'sub')), may hold values from -2 to 2
- normals: float32 [12, 8192], P(None, ('dom', 'sub')), may hold values from -3.5 to 3.5
- bulk_modulus: float32 [8192], P(('dom', 'sub')), may hold values from 0.5 to 2
- density: float32 [8192], P(('dom', 'sub')), may hold values from 0.5 to 2
- deriv_mats: float32 [3, 35, 35], replicated, may hold values from -1 to 1
- face_proj: float32 [4, 15, 35], replicated, may hold values from -1 to 1
- face_lift: float32 [4, 35, 15], replicated, may hold values from -1 to 1
- cluster: int32 [8192], P(('dom', 'sub')), may hold values from 0 to 1, as said below
- pml_flags: int32 [8192], P(('dom', 'sub')), may hold values 0 or 1
- neighbours: int32 [4, 8192], P(None, ('dom', 'sub')), may hold values from 0 to 1343, as said below
- dom_send: int32 [64, 96], P(('dom', 'sub')), may hold values from 0 to 1023, as said below
- sub_send: int32 [128, 32], P(('dom', 'sub')), may hold values from 0 to 1022, as said below
Outputs:
- final_dofs: float32 [140, 8192], P(None, ('dom', 'sub'))
Inputs may be any that keep to these rules, and one draw needn't show every extreme that they name: `cluster`: on every device the fine elements come first among its 256 elements; a device holds at most 64 of them, and some device exactly 64. `neighbours`: each face names one column of its device's trace pool. Own faces that are not listed for sending name each other in pairs. The face at place j of dom_send row 0 names place j of the block from the device before, the one at place j of row 1 place j of the block from the device after; the face at place j of the sub_send row for device b names place j of the block from b, or place j + 1 - 2 (j % 2) when b is the device itself. `dom_send`: together with its sub_send rows, the rows of one device list distinct columns of its own faces; every device lists its last face column here. `sub_send`: together with its dom_send rows, the rows of one device list distinct columns of its own faces; every device lists its second-to-last face column here.
All inputs are finite; a program needn't handle non-finite values. No bound on the sum of `pml_flags` on one device may be relied on, other than what follows from the above.
Results may differ from a plain program's by a relative error of at most 0.0003.
Values sent between devices are 32-bit elements; how exact they have to be, the bound alone decides.
No kernel may reach another device: no remote copies, remote signals or barrier semaphores. Data moves between devices by JAX's collectives and lax.ppermute only.
A program may use at most 64 MiB of HBM per device.

v0:
```python
import math
import jax
import jax.numpy as jnp
from jax import lax
from jax.sharding import PartitionSpec as P

NQ = 4
NB = 35
ORDER = 5
SUBSTEPS = 4
exact_dots = lax.Precision.HIGHEST
step_size = 0.8
sigma_pml = 1.5


def from_behind(shard, axis, by):
    peers = lax.axis_size(axis)
    pairs = [(i, i + by) for i in range(peers) if 0 <= i + by < peers]
    return lax.ppermute(shard, axis, pairs)


def apply_operator(coeffs, material):
    inv_jac, bulk_modulus, density, damping, deriv_mats = material
    n_basis = deriv_mats.shape[1]
    pressure = coeffs[0]
    velocity = coeffs[1:]
    stacked = deriv_mats.reshape(3 * n_basis, n_basis)
    d_press = jnp.dot(stacked, pressure, precision=exact_dots).reshape(3, n_basis, -1)
    jacobian = inv_jac.reshape(3, 3, -1)
    gradient = jnp.sum(jacobian[:, :, None, :] * d_press[:, None, :, :], axis=0)
    mixed_vel = jnp.sum(jacobian[:, :, None, :] * velocity[None, :, :, :], axis=1)
    joined = jnp.transpose(deriv_mats, (1, 0, 2)).reshape(n_basis, 3 * n_basis)
    diverg = jnp.dot(joined, mixed_vel.reshape(3 * n_basis, -1), precision=exact_dots)
    press_rate = -bulk_modulus * diverg - damping * pressure
    veloc_rate = -gradient / density - damping * velocity
    return jnp.concatenate([press_rate[None], veloc_rate], axis=0)


def taylor(coeffs, material):
    deriv_terms = [coeffs]
    for power in range(ORDER - 1):
        deriv_terms.append(apply_operator(deriv_terms[-1], material))
    return deriv_terms


def integrate(deriv_terms, start_time, end_time):
    summed = None
    for power, taylor_term in enumerate(deriv_terms):
        weight = (end_time ** (power + 1) - start_time ** (power + 1)) / math.factorial(power + 1)
        scaled = weight * taylor_term
        summed = scaled if summed is None else summed + scaled
    return summed


def face_traces(coeffs, face_proj):
    face_parts = []
    for face_idx in range(4):
        traced = jnp.einsum("kb,qbe->kqe", face_proj[face_idx], coeffs, precision=exact_dots)
        face_parts.append(traced.reshape(-1, coeffs.shape[2]))
    return jnp.concatenate(face_parts, axis=1)


def corrections(own_traces, nbr_traces, normals, bulk_modulus, density, face_lift):
    n_elem = normals.shape[1]
    n_face = face_lift.shape[2]
    jump_all = (nbr_traces - own_traces).reshape(n_face, 4, 4, n_elem)
    jump_press = jump_all[:, 0]
    jump_vel = jump_all[:, 1:]
    facing = jnp.transpose(normals.reshape(4, 3, n_elem), (1, 0, 2))
    normal_flow = jnp.sum(facing[None] * jump_vel, axis=1)
    sound_speed = jnp.sqrt(bulk_modulus / density)
    penalty = sound_speed * jnp.sqrt(jnp.sum(facing * facing, axis=0))
    flux_press = 0.5 * (bulk_modulus * normal_flow - penalty * jump_press)
    flux_veloc = 0.5 * (facing[None] * jump_press[:, None] / density - penalty * jump_vel)
    flux_all = jnp.concatenate([flux_press[:, None], flux_veloc], axis=1)
    return jnp.einsum("fbk,kqfe->qbe", face_lift, flux_all, precision=exact_dots)


def gather_faces(own_traces, dom_send, sub_send):
    n_chan = own_traces.shape[0]
    n_sub = sub_send.shape[0]
    sub_width = sub_send.shape[1]
    dom_out = jnp.stack(
        [jnp.take(own_traces, dom_send[0], axis=1), jnp.take(own_traces, dom_send[1], axis=1)]
    )
    sub_out = jnp.take(own_traces, sub_send.reshape(-1), axis=1).reshape(n_chan, n_sub, sub_width)
    sub_in = lax.all_to_all(sub_out, "sub", split_axis=1, concat_axis=1, tiled=True).reshape(
        n_chan, n_sub * sub_width
    )
    from_below = from_behind(dom_out[1], "dom", 1)
    from_above = from_behind(dom_out[0], "dom", -1)
    return jnp.concatenate([own_traces, from_below, from_above, sub_in], axis=1)


def body(
    start_dofs,
    inv_jac,
    normals,
    bulk_modulus,
    density,
    deriv_mats,
    face_proj,
    face_lift,
    cluster,
    pml_flags,
    neighbours,
    dom_send,
    sub_send,
):
    n_elem = start_dofs.shape[1]
    dofs_zero = start_dofs.reshape(NQ, NB, n_elem)
    damping = sigma_pml * pml_flags.astype(jnp.float32)
    fine_mask = cluster == 1
    material = (inv_jac, bulk_modulus, density, damping, deriv_mats)
    coarse_terms = taylor(dofs_zero, material)
    sub_dt = step_size / SUBSTEPS
    head_material = (inv_jac, bulk_modulus, density, damping, deriv_mats)
    work_state = jnp.where(fine_mask, dofs_zero, 0.0)
    for sub_step in range(SUBSTEPS):
        coarse_part = integrate(coarse_terms, sub_step * sub_dt, (sub_step + 1) * sub_dt)
        work_head = work_state
        fine_part = integrate(taylor(work_head, head_material), 0.0, sub_dt)
        published = jnp.where(fine_mask, fine_part, coarse_part)
        own_traces = face_traces(published, face_proj)
        trace_pool = gather_faces(own_traces, dom_send, sub_send)
        nbr_traces = jnp.take(trace_pool, neighbours.reshape(-1), axis=1)
        lifted = corrections(own_traces, nbr_traces, normals, bulk_modulus, density, face_lift)
        coarse_next = work_state + lifted
        stepped = work_head + apply_operator(fine_part, head_material) - lifted
        head_next = jnp.where(fine_mask, stepped, coarse_next)
        work_state = head_next
    full_step = integrate(coarse_terms, 0.0, step_size)
    coarse_out = dofs_zero + apply_operator(full_step, material) - work_state
    return jnp.where(fine_mask, work_state, coarse_out).reshape(NQ * NB, n_elem)


def solution(mesh):
    in_specs = (
        P(None, ("dom", "sub")),
        P(None, ("dom", "sub")),
        P(None, ("dom", "sub")),
        P(("dom", "sub")),
        P(("dom", "sub")),
        P(),
        P(),
        P(),
        P(("dom", "sub")),
        P(("dom", "sub")),
        P(None, ("dom", "sub")),
        P(("dom", "sub"), None),
        P(("dom", "sub"), None),
    )
    out_specs = P(None, ("dom", "sub"))
    return jax.shard_map(body, mesh=mesh, in_specs=in_specs, out_specs=out_specs, check_vma=False)
```

profile of v0, /device:TPU:11, one launch (start us, length us, event | category | flops | bytes accessed | tf_op | source)
XLA Modules:
  0.0 125.4 jit_solution(3070285738189939827)
XLA Ops:
  0.0 0.8 reshape.421
  0.8 0.9 reshape.662
  1.7 0.9 slice.126
  2.9 0.6 copy-done.33
  3.7 0.6 copy-done.4
  4.3 0.6 divide_sqrt_fusion
  5.0 0.6 copy-done.2
  7.1 0.8 slice-done
  9.3 0.7 copy-done.13
  10.8 0.8 multiply_reduce_fusion.1
  15.3 0.6 gather_fusion.2
  16.0 0.7 reshape.663
  16.8 4.9 %all-to-all-start = ((f32[4,1,1920]{2,1,0:T(1,128)}), f32[4,1,1920]{2,1,0:T(1,128)S(1)}, u32[]{:S(2)}, u32[]{:S(2)}) async-start(f32[4,1,1920]{2,1,0:T(1,128)} %reshape.663), calls=%async_computation | async-start | bytes 61440 | tf_op jit(solution)/shard_map/all_to_all | solution.py:87
  21.7 0.7 copy-done.29
  22.4 0.6 gather_fusion
  23.1 4.2 %collective-permute-start = (f32[60,96]{0,1:T(8,128)S(1)}, f32[60,96]{0,1:T(8,128)S(1)}, u32[]{:S(2)}, u32[]{:S(2)}) collective-permute-start(f32[60,96]{0,1:T(8,128)S(1)} %select_bitcast_fusion.7), channel_id=1, source_target_pairs={{0,4},{4,8},{8,12},{12,16},{16,20},{20,24},{24,28},{1,5},{5,9},{9,... | collective-permute-start | bytes 69128 | tf_op jit(solution)/shard_map/ppermute | solution.py:19
  27.3 0.6 gather_fusion.1
  28.0 0.7 select_bitcast_fusion.6
  28.7 1.9 %collective-permute-start.1 = (f32[60,96]{0,1:T(8,128)}, f32[60,96]{0,1:T(8,128)}, u32[]{:S(2)}, u32[]{:S(2)}) collective-permute-start(f32[60,96]{0,1:T(8,128)} %select_bitcast_fusion.6), channel_id=1, source_target_pairs={{4,0},{8,4},{12,8},{16,12},{20,16},{24,20},{28,24},{5,1},{9,5},{13... | collective-permute-start | bytes 69128 | tf_op jit(solution)/shard_map/ppermute | solution.py:19
  30.9 0.7 copy-done.19
  32.5 0.6 copy-done.30
  33.2 2.1 %collective-permute-done.1 = f32[60,96]{0,1:T(8,128)} collective-permute-done((f32[60,96]{0,1:T(8,128)}, f32[60,96]{0,1:T(8,128)}, u32[]{:S(2)}, u32[]{:S(2)}) %collective-permute-start.1) | collective-permute-done | bytes 23072 | tf_op jit(solution)/shard_map/ppermute | solution.py:19
  35.3 0.8 constant_dynamic-update-slice_fusion.1
  36.1 0.5 broadcast.471
  36.6 0.6 reduce
  37.4 2.8 %gather_fusion.3 = f32[1024,60]{1,0:T(8,128)S(1)} fusion(f32[60,1344]{0,1:T(8,128)S(1)} %constant_dynamic-update-slice_fusion, s32[1024]{0:T(1024)S(1)} %get-tuple-element.102), kind=kCustom, calls=%fused_computation.2.clone | custom fusion | bytes 495616 | tf_op jit(solution)/shard_map/jit(_take)/gather | solution.py:126
  41.0 0.7 copy-done.5
  46.6 0.7 gather_fusion.5
  47.4 0.7 gather_fusion.4
  48.1 0.8 gather_fusion.6
  49.4 0.6 copy-done.28
  50.1 0.7 reshape.665
  50.9 4.5 %all-to-all-start.1 = ((f32[4,1,1920]{2,1,0:T(1,128)}), f32[4,1,1920]{2,1,0:T(1,128)S(1)}, u32[]{:S(2)}, u32[]{:S(2)}) async-start(f32[4,1,1920]{2,1,0:T(1,128)} %reshape.665), calls=%async_computation.1 | async-start | bytes 61440 | tf_op jit(solution)/shard_map/all_to_all | solution.py:87
  55.4 3.0 %collective-permute-start.2 = (f32[60,96]{0,1:T(8,128)S(1)}, f32[60,96]{0,1:T(8,128)S(1)}, u32[]{:S(2)}, u32[]{:S(2)}) collective-permute-start(f32[60,96]{0,1:T(8,128)S(1)} %select_bitcast_fusion.5), channel_id=1, source_target_pairs={{0,4},{4,8},{8,12},{12,16},{16,20},{20,24},{24,28},{1,5},{5,9},{9,... | collective-permute-start | bytes 69128 | tf_op jit(solution)/shard_map/ppermute | solution.py:19
  58.4 1.9 %collective-permute-start.3 = (f32[60,96]{0,1:T(8,128)S(1)}, f32[60,96]{0,1:T(8,128)S(1)}, u32[]{:S(2)}, u32[]{:S(2)}) collective-permute-start(f32[60,96]{0,1:T(8,128)S(1)} %select_bitcast_fusion.4), channel_id=1, source_target_pairs={{4,0},{8,4},{12,8},{16,12},{20,16},{24,20},{28,24},{5,1},{9,5},{13... | collective-permute-start | bytes 69128 | tf_op jit(solution)/shard_map/ppermute | solution.py:19
  60.4 4.3 %collective-permute-done.3 = f32[60,96]{0,1:T(8,128)S(1)} collective-permute-done((f32[60,96]{0,1:T(8,128)S(1)}, f32[60,96]{0,1:T(8,128)S(1)}, u32[]{:S(2)}, u32[]{:S(2)}) %collective-permute-start.3) | collective-permute-done | bytes 23072 | tf_op jit(solution)/shard_map/ppermute | solution.py:19
  64.7 0.6 reduce.1
  65.5 2.8 %gather_fusion.7 = f32[1024,60]{1,0:T(8,128)S(1)} fusion(f32[60,1344]{0,1:T(8,128)S(1)} %constant_dynamic-update-slice_fusion.7, s32[1024]{0:T(1024)S(1)} %get-tuple-element.102), kind=kCustom, calls=%fused_computation.13.clone | custom fusion | bytes 495616 | tf_op jit(solution)/shard_map/jit(_take)/gather | solution.py:126
  74.1 0.7 gather_fusion.9
  74.8 0.7 gather_fusion.8
  75.6 0.8 gather_fusion.10
  76.7 0.5 copy-done.23
  77.4 0.7 reshape.667
  78.3 4.5 %all-to-all-start.2 = ((f32[4,1,1920]{2,1,0:T(1,128)}), f32[4,1,1920]{2,1,0:T(1,128)S(1)}, u32[]{:S(2)}, u32[]{:S(2)}) async-start(f32[4,1,1920]{2,1,0:T(1,128)} %reshape.667), calls=%async_computation.2 | async-start | bytes 61440 | tf_op jit(solution)/shard_map/all_to_all | solution.py:87
  82.8 2.4 %collective-permute-start.4 = (f32[60,96]{0,1:T(8,128)S(1)}, f32[60,96]{0,1:T(8,128)S(1)}, u32[]{:S(2)}, u32[]{:S(2)}) collective-permute-start(f32[60,96]{0,1:T(8,128)S(1)} %select_bitcast_fusion.3), channel_id=1, source_target_pairs={{0,4},{4,8},{8,12},{12,16},{16,20},{20,24},{24,28},{1,5},{5,9},{9,... | collective-permute-start | bytes 69128 | tf_op jit(solution)/shard_map/ppermute | solution.py:19
  85.3 1.9 %collective-permute-start.5 = (f32[60,96]{0,1:T(8,128)S(1)}, f32[60,96]{0,1:T(8,128)S(1)}, u32[]{:S(2)}, u32[]{:S(2)}) collective-permute-start(f32[60,96]{0,1:T(8,128)S(1)} %select_bitcast_fusion.2), channel_id=1, source_target_pairs={{4,0},{8,4},{12,8},{16,12},{20,16},{24,20},{28,24},{5,1},{9,5},{13... | collective-permute-start | bytes 69128 | tf_op jit(solution)/shard_map/ppermute | solution.py:19
  87.3 4.3 %collective-permute-done.5 = f32[60,96]{0,1:T(8,128)S(1)} collective-permute-done((f32[60,96]{0,1:T(8,128)S(1)}, f32[60,96]{0,1:T(8,128)S(1)}, u32[]{:S(2)}, u32[]{:S(2)}) %collective-permute-start.5) | collective-permute-done | bytes 23072 | tf_op jit(solution)/shard_map/ppermute | solution.py:19
  91.6 0.6 reduce.2
  92.4 2.8 %gather_fusion.11 = f32[1024,60]{1,0:T(8,128)S(1)} fusion(f32[60,1344]{0,1:T(8,128)S(1)} %constant_dynamic-update-slice_fusion.14, s32[1024]{0:T(1024)S(1)} %get-tuple-element.102), kind=kCustom, calls=%fused_computation.14.clone | custom fusion | bytes 495616 | tf_op jit(solution)/shard_map/jit(_take)/gather | solution.py:126
  95.9 0.7 copy-done.15
  99.6 0.5 copy-done.12
  100.4 0.5 copy-done.10
  101.1 0.5 copy-done.8
  103.0 0.7 gather_fusion.13
  103.8 0.7 gather_fusion.12
  104.5 0.8 gather_fusion.14
  106.0 0.7 reshape.669
  106.7 4.5 %all-to-all-start.3 = ((f32[4,1,1920]{2,1,0:T(1,128)}), f32[4,1,1920]{2,1,0:T(1,128)S(1)}, u32[]{:S(2)}, u32[]{:S(2)}) async-start(f32[4,1,1920]{2,1,0:T(1,128)} %reshape.669), calls=%async_computation.3 | async-start | bytes 61440 | tf_op jit(solution)/shard_map/all_to_all | solution.py:87
  111.2 2.4 %collective-permute-start.6 = (f32[60,96]{0,1:T(8,128)S(1)}, f32[60,96]{0,1:T(8,128)S(1)}, u32[]{:S(2)}, u32[]{:S(2)}) collective-permute-start(f32[60,96]{0,1:T(8,128)S(1)} %select_bitcast_fusion.1), channel_id=1, source_target_pairs={{0,4},{4,8},{8,12},{12,16},{16,20},{20,24},{24,28},{1,5},{5,9},{9,... | collective-permute-start | bytes 69128 | tf_op jit(solution)/shard_map/ppermute | solution.py:19
  113.7 1.9 %collective-permute-start.7 = (f32[60,96]{0,1:T(8,128)S(1)}, f32[60,96]{0,1:T(8,128)S(1)}, u32[]{:S(2)}, u32[]{:S(2)}) collective-permute-start(f32[60,96]{0,1:T(8,128)S(1)} %select_bitcast_fusion), channel_id=1, source_target_pairs={{4,0},{8,4},{12,8},{16,12},{20,16},{24,20},{28,24},{5,1},{9,5},{13... | collective-permute-start | bytes 69128 | tf_op jit(solution)/shard_map/ppermute | solution.py:19
  115.7 4.3 %collective-permute-done.7 = f32[60,96]{0,1:T(8,128)S(1)} collective-permute-done((f32[60,96]{0,1:T(8,128)S(1)}, f32[60,96]{0,1:T(8,128)S(1)}, u32[]{:S(2)}, u32[]{:S(2)}) %collective-permute-start.7) | collective-permute-done | bytes 23072 | tf_op jit(solution)/shard_map/ppermute | solution.py:19
  120.0 0.6 reduce.3
  120.8 2.8 %gather_fusion.15 = f32[1024,60]{1,0:T(8,128)S(1)} fusion(f32[60,1344]{0,1:T(8,128)S(1)} %constant_dynamic-update-slice_fusion.21, s32[1024]{0:T(1024)S(1)} %get-tuple-element.102), kind=kCustom, calls=%fused_computation.15.clone | custom fusion | bytes 495616 | tf_op jit(solution)/shard_map/jit(_take)/gather | solution.py:126
  124.7 0.7 reshape.447
  (368 shorter events, 28.5 us)
Async XLA Ops:
  0.8 15.2 %copy-start.27 = (pred[128]{0:T(512)(128)(4,1)}, pred[128]{0:T(512)(128)(4,1)S(1)}, u32[]{:S(2)}) copy-start(pred[128]{0:T(512)(128)(4,1)S(1)} %compare_and_fusion.1) | copy-start | bytes 388
  0.8 1.8 %copy-start.1 = (f32[140,256]{1,0:T(8,128)S(1)}, f32[140,256]{1,0:T(8,128)}, u32[]{:S(2)}) copy-start(f32[140,256]{1,0:T(8,128)} %param.19) | copy-start | bytes 430084
  1.7 0.9 copy-start
  2.9 0.7 copy-start.33
  2.9 0.7 copy-start.18
  3.6 0.7 copy-start.4
  3.6 0.7 copy-start.14
  3.7 0.7 copy-start.32
  5.0 0.7 copy-start.2
  7.0 0.9 slice-start
  9.3 0.8 copy-start.13
  9.3 0.9 copy-start.3
  10.0 5.2 %copy-start.25 = (s32[1024]{0:T(1024)}, s32[1024]{0:T(1024)S(1)}, u32[]{:S(2)}) copy-start(s32[1024]{0:T(1024)S(1)} %pad_clamp_fusion) | copy-start | bytes 12292
  10.1 62.1 %copy-start.11 = (f32[1,15,35]{2,0,1:T(1,128)}, f32[1,15,35]{2,0,1:T(1,128)S(1)}, u32[]{:S(2)}) copy-start(f32[1,15,35]{2,0,1:T(1,128)S(1)} %get-tuple-element.91) | copy-start | bytes 6304
  10.1 62.3 %copy-start.9 = (f32[1,15,35]{2,0,1:T(1,128)}, f32[1,15,35]{2,0,1:T(1,128)S(1)}, u32[]{:S(2)}) copy-start(f32[1,15,35]{2,0,1:T(1,128)S(1)} %get-tuple-element.92) | copy-start | bytes 6304
  10.1 62.5 %copy-start.7 = (f32[1,15,35]{2,0,1:T(1,128)}, f32[1,15,35]{2,0,1:T(1,128)S(1)}, u32[]{:S(2)}) copy-start(f32[1,15,35]{2,0,1:T(1,128)S(1)} %get-tuple-element.93) | copy-start | bytes 6304
  16.8 4.9 %copy-start.31 = (s32[2,96]{1,0:T(2,128)S(1)}, s32[2,96]{1,0:T(2,128)}, u32[]{:S(2)}) copy-start(s32[2,96]{1,0:T(2,128)} %param.30) | copy-start | bytes 2308
  16.8 19.3 %all-to-all-start = ((f32[4,1,1920]{2,1,0:T(1,128)}), f32[4,1,1920]{2,1,0:T(1,128)S(1)}, u32[]{:S(2)}, u32[]{:S(2)}) async-start(f32[4,1,1920]{2,1,0:T(1,128)} %reshape.663), calls=%async_computation | async-start | bytes 61440 | tf_op jit(solution)/shard_map/all_to_all | solution.py:87
  21.6 0.7 copy-start.29
  21.7 27.6 %copy-start.22 = (pred[96]{0:T(512)(128)(4,1)}, pred[96]{0:T(512)(128)(4,1)S(1)}, u32[]{:S(2)}) copy-start(pred[96]{0:T(512)(128)(4,1)S(1)} %get-tuple-element.59) | copy-start | bytes 292
  21.7 29.1 %copy-start.20 = (pred[96]{0:T(512)(128)(4,1)}, pred[96]{0:T(512)(128)(4,1)S(1)}, u32[]{:S(2)}) copy-start(pred[96]{0:T(512)(128)(4,1)S(1)} %get-tuple-element.98) | copy-start | bytes 292
  22.3 0.6 copy-start.24
  23.1 10.1 %collective-permute-start = (f32[60,96]{0,1:T(8,128)S(1)}, f32[60,96]{0,1:T(8,128)S(1)}, u32[]{:S(2)}, u32[]{:S(2)}) collective-permute-start(f32[60,96]{0,1:T(8,128)S(1)} %select_bitcast_fusion.7), channel_id=1, source_target_pairs={{0,4},{4,8},{8,12},{12,16},{16,20},{20,24},{24,28},{1,5},{5,9},{9,... | collective-permute-start | bytes 69128 | tf_op jit(solution)/shard_map/ppermute | solution.py:19
  27.3 0.6 copy-start.26
  28.7 6.6 %collective-permute-start.1 = (f32[60,96]{0,1:T(8,128)}, f32[60,96]{0,1:T(8,128)}, u32[]{:S(2)}, u32[]{:S(2)}) collective-permute-start(f32[60,96]{0,1:T(8,128)} %select_bitcast_fusion.6), channel_id=1, source_target_pairs={{4,0},{8,4},{12,8},{16,12},{20,16},{24,20},{28,24},{5,1},{9,5},{13... | collective-permute-start | bytes 69128 | tf_op jit(solution)/shard_map/ppermute | solution.py:19
  30.6 9.6 %copy-start.16 = (pred[1024]{0:T(1024)(128)(4,1)}, pred[1024]{0:T(1024)(128)(4,1)S(1)}, u32[]{:S(2)}) copy-start(pred[1024]{0:T(1024)(128)(4,1)S(1)} %compare_and_fusion) | copy-start | bytes 3076
  30.9 0.7 copy-start.19
  30.9 0.9 copy-start.6
  32.5 0.6 copy-start.30
  40.9 0.8 copy-start.5
  49.3 0.7 copy-start.28
  50.9 13.8 %all-to-all-start.1 = ((f32[4,1,1920]{2,1,0:T(1,128)}), f32[4,1,1920]{2,1,0:T(1,128)S(1)}, u32[]{:S(2)}, u32[]{:S(2)}) async-start(f32[4,1,1920]{2,1,0:T(1,128)} %reshape.665), calls=%async_computation.1 | async-start | bytes 61440 | tf_op jit(solution)/shard_map/all_to_all | solution.py:87
  55.4 5.0 %collective-permute-start.2 = (f32[60,96]{0,1:T(8,128)S(1)}, f32[60,96]{0,1:T(8,128)S(1)}, u32[]{:S(2)}, u32[]{:S(2)}) collective-permute-start(f32[60,96]{0,1:T(8,128)S(1)} %select_bitcast_fusion.5), channel_id=1, source_target_pairs={{0,4},{4,8},{8,12},{12,16},{16,20},{20,24},{24,28},{1,5},{5,9},{9,... | collective-permute-start | bytes 69128 | tf_op jit(solution)/shard_map/ppermute | solution.py:19
  58.4 6.3 %collective-permute-start.3 = (f32[60,96]{0,1:T(8,128)S(1)}, f32[60,96]{0,1:T(8,128)S(1)}, u32[]{:S(2)}, u32[]{:S(2)}) collective-permute-start(f32[60,96]{0,1:T(8,128)S(1)} %select_bitcast_fusion.4), channel_id=1, source_target_pairs={{4,0},{8,4},{12,8},{16,12},{20,16},{24,20},{28,24},{5,1},{9,5},{13... | collective-permute-start | bytes 69128 | tf_op jit(solution)/shard_map/ppermute | solution.py:19
  65.5 2.8 %copy-start.17 = (pred[1024]{0:T(1024)(128)(4,1)S(1)}, pred[1024]{0:T(1024)(128)(4,1)}, u32[]{:S(2)}) copy-start(pred[1024]{0:T(1024)(128)(4,1)} %copy-done.16) | copy-start | bytes 3076
  76.7 0.6 copy-start.23
  77.4 0.8 copy-start.21
  78.3 13.3 %all-to-all-start.2 = ((f32[4,1,1920]{2,1,0:T(1,128)}), f32[4,1,1920]{2,1,0:T(1,128)S(1)}, u32[]{:S(2)}, u32[]{:S(2)}) async-start(f32[4,1,1920]{2,1,0:T(1,128)} %reshape.667), calls=%async_computation.2 | async-start | bytes 61440 | tf_op jit(solution)/shard_map/all_to_all | solution.py:87
  82.8 4.4 %collective-permute-start.4 = (f32[60,96]{0,1:T(8,128)S(1)}, f32[60,96]{0,1:T(8,128)S(1)}, u32[]{:S(2)}, u32[]{:S(2)}) collective-permute-start(f32[60,96]{0,1:T(8,128)S(1)} %select_bitcast_fusion.3), channel_id=1, source_target_pairs={{0,4},{4,8},{8,12},{12,16},{16,20},{20,24},{24,28},{1,5},{5,9},{9,... | collective-permute-start | bytes 69128 | tf_op jit(solution)/shard_map/ppermute | solution.py:19
  85.3 6.3 %collective-permute-start.5 = (f32[60,96]{0,1:T(8,128)S(1)}, f32[60,96]{0,1:T(8,128)S(1)}, u32[]{:S(2)}, u32[]{:S(2)}) collective-permute-start(f32[60,96]{0,1:T(8,128)S(1)} %select_bitcast_fusion.2), channel_id=1, source_target_pairs={{4,0},{8,4},{12,8},{16,12},{20,16},{24,20},{28,24},{5,1},{9,5},{13... | collective-permute-start | bytes 69128 | tf_op jit(solution)/shard_map/ppermute | solution.py:19
  95.9 0.7 copy-start.15
  99.5 0.7 copy-start.12
  100.2 0.7 copy-start.10
  100.9 0.7 copy-start.8
  106.7 13.3 %all-to-all-start.3 = ((f32[4,1,1920]{2,1,0:T(1,128)}), f32[4,1,1920]{2,1,0:T(1,128)S(1)}, u32[]{:S(2)}, u32[]{:S(2)}) async-start(f32[4,1,1920]{2,1,0:T(1,128)} %reshape.669), calls=%async_computation.3 | async-start | bytes 61440 | tf_op jit(solution)/shard_map/all_to_all | solution.py:87
  111.2 4.4 %collective-permute-start.6 = (f32[60,96]{0,1:T(8,128)S(1)}, f32[60,96]{0,1:T(8,128)S(1)}, u32[]{:S(2)}, u32[]{:S(2)}) collective-permute-start(f32[60,96]{0,1:T(8,128)S(1)} %select_bitcast_fusion.1), channel_id=1, source_target_pairs={{0,4},{4,8},{8,12},{12,16},{16,20},{20,24},{24,28},{1,5},{5,9},{9,... | collective-permute-start | bytes 69128 | tf_op jit(solution)/shard_map/ppermute | solution.py:19
  113.7 6.3 %collective-permute-start.7 = (f32[60,96]{0,1:T(8,128)S(1)}, f32[60,96]{0,1:T(8,128)S(1)}, u32[]{:S(2)}, u32[]{:S(2)}) collective-permute-start(f32[60,96]{0,1:T(8,128)S(1)} %select_bitcast_fusion), channel_id=1, source_target_pairs={{4,0},{8,4},{12,8},{16,12},{20,16},{24,20},{28,24},{5,1},{9,5},{13... | collective-permute-start | bytes 69128 | tf_op jit(solution)/shard_map/ppermute | solution.py:19
where the time goes:
time: 127 us; the launch traced here: 125 us
  local copies, waits for them, and re-layouts  42.8 us (34%)
  starting transfers between devices  38.3 us (30%)
  matrix products  17.1 us (13%)
  waiting for transfers between devices  15 us (12%)
  other arithmetic  9.86 us (8%)
  between operations  2.35 us (2%)
    ppermute x8, starting transfers between devices, from_behind(): return lax.ppermute(shard, axis, pairs)  19.8 us
    all_to_all x4, starting transfers between devices, gather_faces(): lax.all_to_all(sub_out, 'sub', split_axis=1, concat_axis=1, tiled=True)  18.5 us
    ppermute x8, waiting for transfers between devices, from_behind(): return lax.ppermute(shard, axis, pairs)  15 us
    unnamed x105, local copies, waits for them, and re-layouts  13.5 us
    gather x4, local copies, waits for them, and re-layouts, body(): nbr_traces = jnp.take(trace_pool, neighbours.reshape(-1), axis=1)  11.2 us
    dot_general x25, matrix products, apply_operator(): jnp.dot(joined, mixed_vel.reshape(3 * n_basis, -1), precision=exact_dots)  6.34 us
    dot_general x25, matrix products, apply_operator(): jnp.dot(stacked, pressure, precision=exact_dots).reshape(3, n_basis, -1)  5.98 us
    dot_general x16, matrix products, face_traces(): jnp.einsum('kb,qbe->kqe', face_proj[face_idx], coeffs, precision=exact_dots)  3.34 us
  transfers between devices with their start and end apart: 12, of which 4 were waited for; matrix products, arithmetic and copies ran while one was open for 3% of the time, Pallas kernels for 0%

commit v1 on v0

--- a/solution.py
+++ b/solution.py
@@ -11,6 +11,25 @@
 exact_dots = lax.Precision.HIGHEST
 step_size = 0.8
 sigma_pml = 1.5
+
+
+def bind_sites(local_values):
+    lane_axis = "sub"
+    block_out, b_next = (lax.psum(1, axis_name=lane_axis), lax.axis_index(lane_axis))
+    z2 = local_values.shape[1] // block_out
+    v1 = jnp.roll(local_values, -b_next * z2, 1)
+    sides = [lax.slice_in_dim(v1, 0, z2, axis=1)]
+    for it in [*range(1, block_out)]:
+        finding = lax.slice_in_dim(v1, it * z2, (it + 1) * z2, axis=1)
+        sides.append(
+            lax.ppermute(
+                finding,
+                axis_name=lane_axis,
+                perm=[(dd, (dd + it) % block_out) for dd in range(block_out)],
+            )
+        )
+    value_now = jnp.concatenate(sides[::-1], 1)
+    return jnp.roll(value_now, (b_next + 1) * sides[0].shape[1], 1)
 
 
 def from_behind(shard, axis, by):
@@ -84,9 +103,7 @@
         [jnp.take(own_traces, dom_send[0], axis=1), jnp.take(own_traces, dom_send[1], axis=1)]
     )
     sub_out = jnp.take(own_traces, sub_send.reshape(-1), axis=1).reshape(n_chan, n_sub, sub_width)
-    sub_in = lax.all_to_all(sub_out, "sub", split_axis=1, concat_axis=1, tiled=True).reshape(
-        n_chan, n_sub * sub_width
-    )
+    sub_in = bind_sites(sub_out).reshape(n_chan, n_sub * sub_width)
     from_below = from_behind(dom_out[1], "dom", 1)
     from_above = from_behind(dom_out[0], "dom", -1)
     return jnp.concatenate([own_traces, from_below, from_above, sub_in], axis=1)

time: 127 us -> 118 us (0.929)
  local copies, waits for them, and re-layouts: 42.8 us -> 39.2 us
  starting transfers between devices: 38.3 us -> 36.2 us
  other arithmetic: 9.86 us -> 7.93 us
  waiting for transfers between devices: 15 us -> 13.5 us
    all_to_all x4 -> x0, starting transfers between devices: 18.5 us -> none  [gather_faces(): lax.all_to_all(sub_out, 'sub', split_axis=1, concat_axis=1, tiled=True)]
    ppermute x0 -> x12, starting transfers between devices: none -> 14.9 us  [bind_sites(): lax.ppermute(finding, axis_name=lane_axis, perm=[(dd, (dd + it) % block_o...]
    unnamed x105 -> x99, local copies, waits for them, and re-layouts: 13.5 us -> 10.6 us
    all_to_all x4 -> x0, other arithmetic: 2.57 us -> none  [gather_faces(): lax.all_to_all(sub_out, 'sub', split_axis=1, concat_axis=1, tiled=True)]
    ppermute x8, waiting for transfers between devices: 15 us -> 13.5 us  [from_behind(): return lax.ppermute(shard, axis, pairs)]
    ppermute x8, starting transfers between devices: 19.8 us -> 21.2 us  [from_behind(): return lax.ppermute(shard, axis, pairs)]
  transfers between devices with their start and end apart: 12 -> 20, of which waited for: 4 -> 4; matrix products, arithmetic and copies ran while one was open for 3% -> 3% of each run, Pallas kernels for 0% -> 0%
where the time goes in v1:
time: 118 us; the launch traced here: 116 us
  local copies, waits for them, and re-layouts  39.2 us (33%)
  starting transfers between devices  36.2 us (31%)
  matrix products  17.1 us (14%)
  waiting for transfers between devices  13.5 us (11%)
  other arithmetic  7.93 us (7%)
  between operations  2.56 us (2%)
    ppermute x8, starting transfers between devices, from_behind(): return lax.ppermute(shard, axis, pairs)  21.2 us
    ppermute x12, starting transfers between devices, bind_sites(): lax.ppermute(finding, axis_name=lane_axis, perm=[(dd, (dd + it) % block_o...  14.9 us
    ppermute x8, waiting for transfers between devices, from_behind(): return lax.ppermute(shard, axis, pairs)  13.5 us
    gather x4, local copies, waits for them, and re-layouts, body(): nbr_traces = jnp.take(trace_pool, neighbours.reshape(-1), axis=1)  11.2 us
    unnamed x99, local copies, waits for them, and re-layouts  10.6 us
    dot_general x25, matrix products, apply_operator(): jnp.dot(joined, mixed_vel.reshape(3 * n_basis, -1), precision=exact_dots)  6.34 us
    dot_general x25, matrix products, apply_operator(): jnp.dot(stacked, pressure, precision=exact_dots).reshape(3, n_basis, -1)  5.97 us
    dot_general x16, matrix products, face_traces(): jnp.einsum('kb,qbe->kqe', face_proj[face_idx], coeffs, precision=exact_dots)  3.34 us
  transfers between devices with their start and end apart: 20, of which 4 were waited for; matrix products, arithmetic and copies ran while one was open for 3% of the time, Pallas kernels for 0%

profile of v1, /device:TPU:11, one launch (start us, length us, event | category | flops | bytes accessed | tf_op | source)
XLA Modules:
  0.0 116.4 jit_solution(2892027966012171664)
XLA Ops:
  0.0 0.7 copy-done.31
  0.8 0.9 reshape.662
  1.7 0.9 slice.174
  2.9 0.6 copy-done.34
  3.7 0.6 copy-done.4
  4.3 0.6 divide_sqrt_fusion
  5.0 0.6 copy-done.2
  7.1 0.8 slice-done
  9.3 0.7 copy-done.13
  10.8 0.8 multiply_reduce_fusion.1
  15.3 0.6 gather_fusion.2
  16.1 0.6 fusion.215
  16.7 1.3 %collective-permute-start.4 = (f32[60,1,32]{0,2,1:T(8,128)}, f32[60,1,32]{0,2,1:T(8,128)}, u32[]{:S(2)}, u32[]{:S(2)}) collective-permute-start(f32[60,1,32]{0,2,1:T(8,128)} %get-tuple-element.105), channel_id=1, source_target_pairs={{0,1},{1,2},{2,3},{3,0},{4,5},{5,6},{6,7},{7,4},{8,9},{9,10},{10,1... | collective-permute-start | bytes 23048 | tf_op jit(solution)/shard_map/ppermute | solution.py:25
  18.0 1.0 collective-permute-start.3
  19.0 1.5 %collective-permute-start.2 = (f32[60,1,32]{0,2,1:T(8,128)}, f32[60,1,32]{0,2,1:T(8,128)}, u32[]{:S(2)}, u32[]{:S(2)}) collective-permute-start(f32[60,1,32]{0,2,1:T(8,128)} %get-tuple-element.107), channel_id=1, source_target_pairs={{0,3},{1,0},{2,1},{3,2},{4,7},{5,4},{6,5},{7,6},{8,11},{9,8},{10,9... | collective-permute-start | bytes 23048 | tf_op jit(solution)/shard_map/ppermute | solution.py:25
  20.5 0.6 gather_fusion
  21.3 4.5 %collective-permute-start = (f32[60,96]{0,1:T(8,128)S(1)}, f32[60,96]{0,1:T(8,128)S(1)}, u32[]{:S(2)}, u32[]{:S(2)}) collective-permute-start(f32[60,96]{0,1:T(8,128)S(1)} %select_bitcast_fusion.7), channel_id=1, source_target_pairs={{0,4},{4,8},{8,12},{12,16},{16,20},{20,24},{24,28},{1,5},{5,9},{9,... | collective-permute-start | bytes 69128 | tf_op jit(solution)/shard_map/ppermute | solution.py:38
  25.8 0.6 gather_fusion.1
  26.5 1.9 %collective-permute-start.1 = (f32[60,96]{0,1:T(8,128)S(1)}, f32[60,96]{0,1:T(8,128)}, u32[]{:S(2)}, u32[]{:S(2)}) collective-permute-start(f32[60,96]{0,1:T(8,128)S(1)} %select_bitcast_fusion.6), channel_id=1, source_target_pairs={{4,0},{8,4},{12,8},{16,12},{20,16},{24,20},{28,24},{5,1},{9,5},{13... | collective-permute-start | bytes 69128 | tf_op jit(solution)/shard_map/ppermute | solution.py:38
  28.8 0.7 copy-done.19
  30.3 0.6 copy-done.30
  31.1 0.9 fusion.152
  32.0 0.9 collective-permute-done.1
  32.9 0.8 constant_dynamic-update-slice_fusion.1
  33.8 2.8 %gather_fusion.3 = f32[1024,60]{1,0:T(8,128)S(1)} fusion(f32[60,1344]{0,1:T(8,128)S(1)} %constant_dynamic-update-slice_fusion, s32[1024]{0:T(1024)S(1)} %get-tuple-element.119), kind=kCustom, calls=%fused_computation.2.clone | custom fusion | bytes 495616 | tf_op jit(solution)/shard_map/jit(_take)/gather | solution.py:143
  37.3 0.7 copy-done.5
  38.0 0.3 fusion.98
  43.0 0.7 gather_fusion.5
  43.7 0.6 gather_fusion.4
  44.4 0.8 gather_fusion.6
  45.6 0.5 copy-done.28
  46.6 3.1 %collective-permute-start.8 = (f32[60,1,32]{0,2,1:T(8,128)S(1)}, f32[60,1,32]{0,2,1:T(8,128)S(1)}, u32[]{:S(2)}, u32[]{:S(2)}) collective-permute-start(f32[60,1,32]{0,2,1:T(8,128)S(1)} %get-tuple-element.102), channel_id=1, source_target_pairs={{0,2},{1,3},{2,0},{3,1},{4,6},{5,7},{6,4},{7,5},{8,10},{9,11},{10,... | collective-permute-start | bytes 23048 | tf_op jit(solution)/shard_map/ppermute | solution.py:25
  49.8 4.2 %collective-permute-start.5 = (f32[60,96]{0,1:T(8,128)S(1)}, f32[60,96]{0,1:T(8,128)S(1)}, u32[]{:S(2)}, u32[]{:S(2)}) collective-permute-start(f32[60,96]{0,1:T(8,128)S(1)} %select_bitcast_fusion.5), channel_id=1, source_target_pairs={{0,4},{4,8},{8,12},{12,16},{16,20},{20,24},{24,28},{1,5},{5,9},{9,... | collective-permute-start | bytes 69128 | tf_op jit(solution)/shard_map/ppermute | solution.py:38
  53.9 1.9 %collective-permute-start.6 = (f32[60,96]{0,1:T(8,128)S(1)}, f32[60,96]{0,1:T(8,128)S(1)}, u32[]{:S(2)}, u32[]{:S(2)}) collective-permute-start(f32[60,96]{0,1:T(8,128)S(1)} %select_bitcast_fusion.4), channel_id=1, source_target_pairs={{4,0},{8,4},{12,8},{16,12},{20,16},{24,20},{28,24},{5,1},{9,5},{13... | collective-permute-start | bytes 69128 | tf_op jit(solution)/shard_map/ppermute | solution.py:38
  56.1 4.2 %collective-permute-done.6 = f32[60,96]{0,1:T(8,128)S(1)} collective-permute-done((f32[60,96]{0,1:T(8,128)S(1)}, f32[60,96]{0,1:T(8,128)S(1)}, u32[]{:S(2)}, u32[]{:S(2)}) %collective-permute-start.6) | collective-permute-done | bytes 23072 | tf_op jit(solution)/shard_map/ppermute | solution.py:38
  60.2 2.8 %gather_fusion.7 = f32[1024,60]{1,0:T(8,128)S(1)} fusion(f32[60,1344]{0,1:T(8,128)S(1)} %constant_dynamic-update-slice_fusion.7, s32[1024]{0:T(1024)S(1)} %get-tuple-element.119), kind=kCustom, calls=%fused_computation.13.clone | custom fusion | bytes 495616 | tf_op jit(solution)/shard_map/jit(_take)/gather | solution.py:143
  63.8 0.3 fusion.104
  68.8 0.7 gather_fusion.9
  69.5 0.7 gather_fusion.8
  70.3 0.8 gather_fusion.10
  71.4 0.6 copy-done.23
  72.4 1.8 %collective-permute-start.14 = (f32[60,1,32]{0,2,1:T(8,128)S(1)}, f32[60,1,32]{0,2,1:T(8,128)S(1)}, u32[]{:S(2)}, u32[]{:S(2)}) collective-permute-start(f32[60,1,32]{0,2,1:T(8,128)S(1)} %get-tuple-element.97), channel_id=1, source_target_pairs={{0,1},{1,2},{2,3},{3,0},{4,5},{5,6},{6,7},{7,4},{8,9},{9,10},{10,1... | collective-permute-start | bytes 23048 | tf_op jit(solution)/shard_map/ppermute | solution.py:25
  74.2 1.5 %collective-permute-start.13 = (f32[60,1,32]{0,2,1:T(8,128)S(1)}, f32[60,1,32]{0,2,1:T(8,128)S(1)}, u32[]{:S(2)}, u32[]{:S(2)}) collective-permute-start(f32[60,1,32]{0,2,1:T(8,128)S(1)} %get-tuple-element.98), channel_id=1, source_target_pairs={{0,2},{1,3},{2,0},{3,1},{4,6},{5,7},{6,4},{7,5},{8,10},{9,11},{10,... | collective-permute-start | bytes 23048 | tf_op jit(solution)/shard_map/ppermute | solution.py:25
  75.7 2.4 %collective-permute-start.10 = (f32[60,96]{0,1:T(8,128)S(1)}, f32[60,96]{0,1:T(8,128)S(1)}, u32[]{:S(2)}, u32[]{:S(2)}) collective-permute-start(f32[60,96]{0,1:T(8,128)S(1)} %select_bitcast_fusion.3), channel_id=1, source_target_pairs={{0,4},{4,8},{8,12},{12,16},{16,20},{20,24},{24,28},{1,5},{5,9},{9,... | collective-permute-start | bytes 69128 | tf_op jit(solution)/shard_map/ppermute | solution.py:38
  78.2 1.9 %collective-permute-start.11 = (f32[60,96]{0,1:T(8,128)S(1)}, f32[60,96]{0,1:T(8,128)S(1)}, u32[]{:S(2)}, u32[]{:S(2)}) collective-permute-start(f32[60,96]{0,1:T(8,128)S(1)} %select_bitcast_fusion.2), channel_id=1, source_target_pairs={{4,0},{8,4},{12,8},{16,12},{20,16},{24,20},{28,24},{5,1},{9,5},{13... | collective-permute-start | bytes 69128 | tf_op jit(solution)/shard_map/ppermute | solution.py:38
  80.3 4.2 %collective-permute-done.11 = f32[60,96]{0,1:T(8,128)S(1)} collective-permute-done((f32[60,96]{0,1:T(8,128)S(1)}, f32[60,96]{0,1:T(8,128)S(1)}, u32[]{:S(2)}, u32[]{:S(2)}) %collective-permute-start.11) | collective-permute-done | bytes 23072 | tf_op jit(solution)/shard_map/ppermute | solution.py:38
  84.5 2.8 %gather_fusion.11 = f32[1024,60]{1,0:T(8,128)S(1)} fusion(f32[60,1344]{0,1:T(8,128)S(1)} %constant_dynamic-update-slice_fusion.14, s32[1024]{0:T(1024)S(1)} %get-tuple-element.119), kind=kCustom, calls=%fused_computation.14.clone | custom fusion | bytes 495616 | tf_op jit(solution)/shard_map/jit(_take)/gather | solution.py:143
  88.0 0.7 copy-done.15
  88.7 0.3 fusion.110
  91.8 0.5 copy-done.12
  92.5 0.5 copy-done.10
  93.2 0.5 copy-done.8
  95.2 0.7 gather_fusion.13
  95.9 0.7 gather_fusion.12
  96.7 0.8 gather_fusion.14
  98.0 0.5 copy-done.21
  98.6 1.8 %collective-permute-start.19 = (f32[60,1,32]{0,2,1:T(8,128)S(1)}, f32[60,1,32]{0,2,1:T(8,128)S(1)}, u32[]{:S(2)}, u32[]{:S(2)}) collective-permute-start(f32[60,1,32]{0,2,1:T(8,128)S(1)} %get-tuple-element.93), channel_id=1, source_target_pairs={{0,1},{1,2},{2,3},{3,0},{4,5},{5,6},{6,7},{7,4},{8,9},{9,10},{10,1... | collective-permute-start | bytes 23048 | tf_op jit(solution)/shard_map/ppermute | solution.py:25
  100.4 2.6 %collective-permute-start.18 = (f32[60,1,32]{0,2,1:T(8,128)S(1)}, f32[60,1,32]{0,2,1:T(8,128)S(1)}, u32[]{:S(2)}, u32[]{:S(2)}) collective-permute-start(f32[60,1,32]{0,2,1:T(8,128)S(1)} %get-tuple-element.94), channel_id=1, source_target_pairs={{0,2},{1,3},{2,0},{3,1},{4,6},{5,7},{6,4},{7,5},{8,10},{9,11},{10,... | collective-permute-start | bytes 23048 | tf_op jit(solution)/shard_map/ppermute | solution.py:25
  103.1 2.4 %collective-permute-start.15 = (f32[60,96]{0,1:T(8,128)S(1)}, f32[60,96]{0,1:T(8,128)S(1)}, u32[]{:S(2)}, u32[]{:S(2)}) collective-permute-start(f32[60,96]{0,1:T(8,128)S(1)} %select_bitcast_fusion.1), channel_id=1, source_target_pairs={{0,4},{4,8},{8,12},{12,16},{16,20},{20,24},{24,28},{1,5},{5,9},{9,... | collective-permute-start | bytes 69128 | tf_op jit(solution)/shard_map/ppermute | solution.py:38
  105.5 1.9 %collective-permute-start.16 = (f32[60,96]{0,1:T(8,128)S(1)}, f32[60,96]{0,1:T(8,128)S(1)}, u32[]{:S(2)}, u32[]{:S(2)}) collective-permute-start(f32[60,96]{0,1:T(8,128)S(1)} %select_bitcast_fusion), channel_id=1, source_target_pairs={{4,0},{8,4},{12,8},{16,12},{20,16},{24,20},{28,24},{5,1},{9,5},{13... | collective-permute-start | bytes 69128 | tf_op jit(solution)/shard_map/ppermute | solution.py:38
  107.7 4.2 %collective-permute-done.16 = f32[60,96]{0,1:T(8,128)S(1)} collective-permute-done((f32[60,96]{0,1:T(8,128)S(1)}, f32[60,96]{0,1:T(8,128)S(1)}, u32[]{:S(2)}, u32[]{:S(2)}) %collective-permute-start.16) | collective-permute-done | bytes 23072 | tf_op jit(solution)/shard_map/ppermute | solution.py:38
  111.9 2.8 %gather_fusion.15 = f32[1024,60]{1,0:T(8,128)S(1)} fusion(f32[60,1344]{0,1:T(8,128)S(1)} %constant_dynamic-update-slice_fusion.21, s32[1024]{0:T(1024)S(1)} %get-tuple-element.119), kind=kCustom, calls=%fused_computation.15.clone | custom fusion | bytes 495616 | tf_op jit(solution)/shard_map/jit(_take)/gather | solution.py:143
  115.4 0.4 subtract_select_fusion
  115.8 0.7 reshape.447
  (385 shorter events, 27.4 us)
Async XLA Ops:
  0.0 0.7 copy-start.31
  0.8 15.1 %copy-start.27 = (pred[128]{0:T(512)(128)(4,1)}, pred[128]{0:T(512)(128)(4,1)S(1)}, u32[]{:S(2)}) copy-start(pred[128]{0:T(512)(128)(4,1)S(1)} %compare_and_fusion.1) | copy-start | bytes 388
  0.8 1.8 %copy-start.1 = (f32[140,256]{1,0:T(8,128)S(1)}, f32[140,256]{1,0:T(8,128)}, u32[]{:S(2)}) copy-start(f32[140,256]{1,0:T(8,128)} %param.21) | copy-start | bytes 430084
  1.7 0.9 copy-start
  2.9 0.7 copy-start.34
  2.9 0.7 copy-start.18
  3.6 0.7 copy-start.4
  3.6 0.7 copy-start.14
  3.7 0.7 copy-start.33
  5.0 0.7 copy-start.2
  7.0 0.9 slice-start
  9.3 0.8 copy-start.13
  9.3 0.9 copy-start.3
  10.0 5.2 %copy-start.25 = (s32[1024]{0:T(1024)}, s32[1024]{0:T(1024)S(1)}, u32[]{:S(2)}) copy-start(s32[1024]{0:T(1024)S(1)} %pad_clamp_fusion) | copy-start | bytes 12292
  10.1 56.8 %copy-start.11 = (f32[1,15,35]{2,0,1:T(1,128)}, f32[1,15,35]{2,0,1:T(1,128)S(1)}, u32[]{:S(2)}) copy-start(f32[1,15,35]{2,0,1:T(1,128)S(1)} %get-tuple-element.108) | copy-start | bytes 6304
  10.1 57.0 %copy-start.9 = (f32[1,15,35]{2,0,1:T(1,128)}, f32[1,15,35]{2,0,1:T(1,128)S(1)}, u32[]{:S(2)}) copy-start(f32[1,15,35]{2,0,1:T(1,128)S(1)} %get-tuple-element.109) | copy-start | bytes 6304
  10.1 57.2 %copy-start.7 = (f32[1,15,35]{2,0,1:T(1,128)}, f32[1,15,35]{2,0,1:T(1,128)S(1)}, u32[]{:S(2)}) copy-start(f32[1,15,35]{2,0,1:T(1,128)S(1)} %get-tuple-element.110) | copy-start | bytes 6304
  15.9 4.5 %copy-start.32 = (s32[2,96]{1,0:T(2,128)S(1)}, s32[2,96]{1,0:T(2,128)}, u32[]{:S(2)}) copy-start(s32[2,96]{1,0:T(2,128)} %param.32) | copy-start | bytes 2308
  16.7 3.8 %copy-start.29 = (s32[4,256]{1,0:T(4,128)S(1)}, s32[4,256]{1,0:T(4,128)}, u32[]{:S(2)}) copy-start(s32[4,256]{1,0:T(4,128)} %param.31) | copy-start | bytes 12292
  16.7 14.4 %collective-permute-start.4 = (f32[60,1,32]{0,2,1:T(8,128)}, f32[60,1,32]{0,2,1:T(8,128)}, u32[]{:S(2)}, u32[]{:S(2)}) collective-permute-start(f32[60,1,32]{0,2,1:T(8,128)} %get-tuple-element.105), channel_id=1, source_target_pairs={{0,1},{1,2},{2,3},{3,0},{4,5},{5,6},{6,7},{7,4},{8,9},{9,10},{10,1... | collective-permute-start | bytes 23048 | tf_op jit(solution)/shard_map/ppermute | solution.py:25
  18.0 13.1 %collective-permute-start.3 = (f32[60,1,32]{0,2,1:T(8,128)}, f32[60,1,32]{0,2,1:T(8,128)}, u32[]{:S(2)}, u32[]{:S(2)}) collective-permute-start(f32[60,1,32]{0,2,1:T(8,128)} %get-tuple-element.106), channel_id=1, source_target_pairs={{0,2},{1,3},{2,0},{3,1},{4,6},{5,7},{6,4},{7,5},{8,10},{9,11},{10,... | collective-permute-start | bytes 23048 | tf_op jit(solution)/shard_map/ppermute | solution.py:25
  19.0 12.1 %collective-permute-start.2 = (f32[60,1,32]{0,2,1:T(8,128)}, f32[60,1,32]{0,2,1:T(8,128)}, u32[]{:S(2)}, u32[]{:S(2)}) collective-permute-start(f32[60,1,32]{0,2,1:T(8,128)} %get-tuple-element.107), channel_id=1, source_target_pairs={{0,3},{1,0},{2,1},{3,2},{4,7},{5,4},{6,5},{7,6},{8,11},{9,8},{10,9... | collective-permute-start | bytes 23048 | tf_op jit(solution)/shard_map/ppermute | solution.py:25
  20.5 25.0 %copy-start.22 = (pred[96]{0:T(512)(128)(4,1)}, pred[96]{0:T(512)(128)(4,1)S(1)}, u32[]{:S(2)}) copy-start(pred[96]{0:T(512)(128)(4,1)S(1)} %get-tuple-element.60) | copy-start | bytes 292
  20.5 51.8 %copy-start.20 = (pred[96]{0:T(512)(128)(4,1)}, pred[96]{0:T(512)(128)(4,1)S(1)}, u32[]{:S(2)}) copy-start(pred[96]{0:T(512)(128)(4,1)S(1)} %get-tuple-element.115) | copy-start | bytes 292
  20.5 23.2 %copy-start.24 = (s32[1024]{0:T(1024)}, s32[1024]{0:T(1024)S(1)}, u32[]{:S(2)}) copy-start(s32[1024]{0:T(1024)S(1)} %get-tuple-element.118) | copy-start | bytes 12292
  21.3 10.7 %collective-permute-start = (f32[60,96]{0,1:T(8,128)S(1)}, f32[60,96]{0,1:T(8,128)S(1)}, u32[]{:S(2)}, u32[]{:S(2)}) collective-permute-start(f32[60,96]{0,1:T(8,128)S(1)} %select_bitcast_fusion.7), channel_id=1, source_target_pairs={{0,4},{4,8},{8,12},{12,16},{16,20},{20,24},{24,28},{1,5},{5,9},{9,... | collective-permute-start | bytes 69128 | tf_op jit(solution)/shard_map/ppermute | solution.py:38
  25.8 0.6 copy-start.26
  26.5 6.4 %collective-permute-start.1 = (f32[60,96]{0,1:T(8,128)S(1)}, f32[60,96]{0,1:T(8,128)}, u32[]{:S(2)}, u32[]{:S(2)}) collective-permute-start(f32[60,96]{0,1:T(8,128)S(1)} %select_bitcast_fusion.6), channel_id=1, source_target_pairs={{4,0},{8,4},{12,8},{16,12},{20,16},{24,20},{28,24},{5,1},{9,5},{13... | collective-permute-start | bytes 69128 | tf_op jit(solution)/shard_map/ppermute | solution.py:38
  28.5 58.8 %copy-start.16 = (pred[1024]{0:T(1024)(128)(4,1)}, pred[1024]{0:T(1024)(128)(4,1)S(1)}, u32[]{:S(2)}) copy-start(pred[1024]{0:T(1024)(128)(4,1)S(1)} %compare_and_fusion) | copy-start | bytes 3076
  28.7 0.7 copy-start.19
  28.8 0.9 copy-start.6
  30.3 0.6 copy-start.30
  37.3 0.8 copy-start.5
  45.5 0.6 copy-start.28
  46.4 9.5 %collective-permute-start.9 = (f32[60,1,32]{0,2,1:T(8,128)S(1)}, f32[60,1,32]{0,2,1:T(8,128)S(1)}, u32[]{:S(2)}, u32[]{:S(2)}) collective-permute-start(f32[60,1,32]{0,2,1:T(8,128)S(1)} %get-tuple-element.101), channel_id=1, source_target_pairs={{0,1},{1,2},{2,3},{3,0},{4,5},{5,6},{6,7},{7,4},{8,9},{9,10},{10,1... | collective-permute-start | bytes 23048 | tf_op jit(solution)/shard_map/ppermute | solution.py:25
  46.6 9.3 %collective-permute-start.8 = (f32[60,1,32]{0,2,1:T(8,128)S(1)}, f32[60,1,32]{0,2,1:T(8,128)S(1)}, u32[]{:S(2)}, u32[]{:S(2)}) collective-permute-start(f32[60,1,32]{0,2,1:T(8,128)S(1)} %get-tuple-element.102), channel_id=1, source_target_pairs={{0,2},{1,3},{2,0},{3,1},{4,6},{5,7},{6,4},{7,5},{8,10},{9,11},{10,... | collective-permute-start | bytes 23048 | tf_op jit(solution)/shard_map/ppermute | solution.py:25
  49.8 6.2 %collective-permute-start.7 = (f32[60,1,32]{0,2,1:T(8,128)S(1)}, f32[60,1,32]{0,2,1:T(8,128)S(1)}, u32[]{:S(2)}, u32[]{:S(2)}) collective-permute-start(f32[60,1,32]{0,2,1:T(8,128)S(1)} %get-tuple-element.103), channel_id=1, source_target_pairs={{0,3},{1,0},{2,1},{3,2},{4,7},{5,4},{6,5},{7,6},{8,11},{9,8},{10,9... | collective-permute-start | bytes 23048 | tf_op jit(solution)/shard_map/ppermute | solution.py:25
  49.8 6.3 %collective-permute-start.5 = (f32[60,96]{0,1:T(8,128)S(1)}, f32[60,96]{0,1:T(8,128)S(1)}, u32[]{:S(2)}, u32[]{:S(2)}) collective-permute-start(f32[60,96]{0,1:T(8,128)S(1)} %select_bitcast_fusion.5), channel_id=1, source_target_pairs={{0,4},{4,8},{8,12},{12,16},{16,20},{20,24},{24,28},{1,5},{5,9},{9,... | collective-permute-start | bytes 69128 | tf_op jit(solution)/shard_map/ppermute | solution.py:38
  53.9 6.3 %collective-permute-start.6 = (f32[60,96]{0,1:T(8,128)S(1)}, f32[60,96]{0,1:T(8,128)S(1)}, u32[]{:S(2)}, u32[]{:S(2)}) collective-permute-start(f32[60,96]{0,1:T(8,128)S(1)} %select_bitcast_fusion.4), channel_id=1, source_target_pairs={{4,0},{8,4},{12,8},{16,12},{20,16},{24,20},{28,24},{5,1},{9,5},{13... | collective-permute-start | bytes 69128 | tf_op jit(solution)/shard_map/ppermute | solution.py:38
  71.4 0.7 copy-start.23
  72.4 7.8 %collective-permute-start.14 = (f32[60,1,32]{0,2,1:T(8,128)S(1)}, f32[60,1,32]{0,2,1:T(8,128)S(1)}, u32[]{:S(2)}, u32[]{:S(2)}) collective-permute-start(f32[60,1,32]{0,2,1:T(8,128)S(1)} %get-tuple-element.97), channel_id=1, source_target_pairs={{0,1},{1,2},{2,3},{3,0},{4,5},{5,6},{6,7},{7,4},{8,9},{9,10},{10,1... | collective-permute-start | bytes 23048 | tf_op jit(solution)/shard_map/ppermute | solution.py:25
  74.2 6.0 %collective-permute-start.13 = (f32[60,1,32]{0,2,1:T(8,128)S(1)}, f32[60,1,32]{0,2,1:T(8,128)S(1)}, u32[]{:S(2)}, u32[]{:S(2)}) collective-permute-start(f32[60,1,32]{0,2,1:T(8,128)S(1)} %get-tuple-element.98), channel_id=1, source_target_pairs={{0,2},{1,3},{2,0},{3,1},{4,6},{5,7},{6,4},{7,5},{8,10},{9,11},{10,... | collective-permute-start | bytes 23048 | tf_op jit(solution)/shard_map/ppermute | solution.py:25
  75.7 4.5 %collective-permute-start.12 = (f32[60,1,32]{0,2,1:T(8,128)S(1)}, f32[60,1,32]{0,2,1:T(8,128)S(1)}, u32[]{:S(2)}, u32[]{:S(2)}) collective-permute-start(f32[60,1,32]{0,2,1:T(8,128)S(1)} %get-tuple-element.99), channel_id=1, source_target_pairs={{0,3},{1,0},{2,1},{3,2},{4,7},{5,4},{6,5},{7,6},{8,11},{9,8},{10,9... | collective-permute-start | bytes 23048 | tf_op jit(solution)/shard_map/ppermute | solution.py:25
  75.7 4.6 %collective-permute-start.10 = (f32[60,96]{0,1:T(8,128)S(1)}, f32[60,96]{0,1:T(8,128)S(1)}, u32[]{:S(2)}, u32[]{:S(2)}) collective-permute-start(f32[60,96]{0,1:T(8,128)S(1)} %select_bitcast_fusion.3), channel_id=1, source_target_pairs={{0,4},{4,8},{8,12},{12,16},{16,20},{20,24},{24,28},{1,5},{5,9},{9,... | collective-permute-start | bytes 69128 | tf_op jit(solution)/shard_map/ppermute | solution.py:38
  78.2 6.3 %collective-permute-start.11 = (f32[60,96]{0,1:T(8,128)S(1)}, f32[60,96]{0,1:T(8,128)S(1)}, u32[]{:S(2)}, u32[]{:S(2)}) collective-permute-start(f32[60,96]{0,1:T(8,128)S(1)} %select_bitcast_fusion.2), channel_id=1, source_target_pairs={{4,0},{8,4},{12,8},{16,12},{20,16},{24,20},{28,24},{5,1},{9,5},{13... | collective-permute-start | bytes 69128 | tf_op jit(solution)/shard_map/ppermute | solution.py:38
  88.0 0.7 copy-start.15
  91.6 0.7 copy-start.12
  92.3 0.7 copy-start.10
  93.0 0.7 copy-start.8
  97.9 0.6 copy-start.21
  98.6 8.9 %collective-permute-start.19 = (f32[60,1,32]{0,2,1:T(8,128)S(1)}, f32[60,1,32]{0,2,1:T(8,128)S(1)}, u32[]{:S(2)}, u32[]{:S(2)}) collective-permute-start(f32[60,1,32]{0,2,1:T(8,128)S(1)} %get-tuple-element.93), channel_id=1, source_target_pairs={{0,1},{1,2},{2,3},{3,0},{4,5},{5,6},{6,7},{7,4},{8,9},{9,10},{10,1... | collective-permute-start | bytes 23048 | tf_op jit(solution)/shard_map/ppermute | solution.py:25
  100.4 7.1 %collective-permute-start.18 = (f32[60,1,32]{0,2,1:T(8,128)S(1)}, f32[60,1,32]{0,2,1:T(8,128)S(1)}, u32[]{:S(2)}, u32[]{:S(2)}) collective-permute-start(f32[60,1,32]{0,2,1:T(8,128)S(1)} %get-tuple-element.94), channel_id=1, source_target_pairs={{0,2},{1,3},{2,0},{3,1},{4,6},{5,7},{6,4},{7,5},{8,10},{9,11},{10,... | collective-permute-start | bytes 23048 | tf_op jit(solution)/shard_map/ppermute | solution.py:25
  103.1 4.5 %collective-permute-start.17 = (f32[60,1,32]{0,2,1:T(8,128)S(1)}, f32[60,1,32]{0,2,1:T(8,128)S(1)}, u32[]{:S(2)}, u32[]{:S(2)}) collective-permute-start(f32[60,1,32]{0,2,1:T(8,128)S(1)} %get-tuple-element.95), channel_id=1, source_target_pairs={{0,3},{1,0},{2,1},{3,2},{4,7},{5,4},{6,5},{7,6},{8,11},{9,8},{10,9... | collective-permute-start | bytes 23048 | tf_op jit(solution)/shard_map/ppermute | solution.py:25
  103.1 4.6 %collective-permute-start.15 = (f32[60,96]{0,1:T(8,128)S(1)}, f32[60,96]{0,1:T(8,128)S(1)}, u32[]{:S(2)}, u32[]{:S(2)}) collective-permute-start(f32[60,96]{0,1:T(8,128)S(1)} %select_bitcast_fusion.1), channel_id=1, source_target_pairs={{0,4},{4,8},{8,12},{12,16},{16,20},{20,24},{24,28},{1,5},{5,9},{9,... | collective-permute-start | bytes 69128 | tf_op jit(solution)/shard_map/ppermute | solution.py:38
  105.5 6.3 %collective-permute-start.16 = (f32[60,96]{0,1:T(8,128)S(1)}, f32[60,96]{0,1:T(8,128)S(1)}, u32[]{:S(2)}, u32[]{:S(2)}) collective-permute-start(f32[60,96]{0,1:T(8,128)S(1)} %select_bitcast_fusion), channel_id=1, source_target_pairs={{4,0},{8,4},{12,8},{16,12},{20,16},{24,20},{28,24},{5,1},{9,5},{13... | collective-permute-start | bytes 69128 | tf_op jit(solution)/shard_map/ppermute | solution.py:38
  111.8 2.8 %copy-start.17 = (pred[1024]{0:T(1024)(128)(4,1)S(1)}, pred[1024]{0:T(1024)(128)(4,1)}, u32[]{:S(2)}) copy-start(pred[1024]{0:T(1024)(128)(4,1)} %copy-done.16) | copy-start | bytes 3076
